TPU v7x, 512 devices: a whole 4x4x16 slice. The times are simulated.
512 devices in a mesh: voxel: 32 (over x, z_lo, core), feature: 4 (over z_hi), tm: 4 (over y).
Axes of the slice: x: 4, y: 4, z: 16 (z_hi: 4, z_lo: 4; z = z_hi * 4 + z_lo), core: 2. Of those that a mesh axis runs over, the one named last changes fastest.
Arguments:
- hidden: bfloat16 [3072, 8192], P('tm', 'feature'), may hold values from -6 to 6
- bold: bfloat16 [3072, 4096], P('tm', 'voxel'), may hold values from -6 to 6
- panel: bfloat16 [65536, 128], P(('feature', 'tm'), 'voxel'), may hold values from -0.0234375 to 0.0234375
- eigvals: float32 [128], replicated, may hold values from 0.05 to 2
- ridge_grid: int32 [24], replicated, may hold values from 0 to 16
- delays: int32 [8], replicated, may hold values from 1 to 12, as said below
- runs: int32 [3072], replicated, may hold values from 0 to 7, never falling along the last dimension, each value on 1 to 768 neighbouring positions
Outputs:
- scaled: bfloat16 [24, 128, 4096], P(None, None, 'voxel')
Inputs may be any that keep to these rules, and one draw needn't show every extreme that they name: 8 distinct delays, 12 among them. `runs`: run numbers never fall along the TRs; a run holds 1 to 768 TRs.
All inputs are finite; a program needn't handle non-finite values.
Results may differ from a plain program's by a relative error of at most 0.022.
Values may be sent and summed in bfloat16 or wider, within the bound.
A program may use at most 64 MiB of HBM per device.

v0:
```python
import math

import jax
import jax.numpy as jnp
from jax import lax
from jax.sharding import PartitionSpec as P

DELAYS = 8
MAXD = 12


def passed_along(value, axis, steps):
    count = lax.axis_size(axis)
    first, last = (max(0, -steps), min(count, count - steps))
    return lax.ppermute(value, axis, [(source, source + steps) for source in range(first, last)])


def contract_rows(left, right):
    return lax.dot_general(
        left, right, (((0,), (0,)), ((), ())), preferred_element_type=jnp.float32
    )


def shards(hidden, bold, panel, eigvals, ridge_grid, delays, runs):
    t_rows = hidden.shape[0]
    d_local = hidden.shape[1]
    v_cols = bold.shape[1]
    total_rows = t_rows * lax.axis_size("tm")
    first = lax.axis_index("tm") * t_rows
    ahead = passed_along(bold[:MAXD], "tm", -1)
    extended = jnp.concatenate([bold, ahead], 0)
    runs_pad = jnp.concatenate([runs, jnp.full((MAXD,), -1, jnp.int32)])
    own_runs = lax.dynamic_slice_in_dim(runs, first, t_rows)
    positions = first + jnp.arange(t_rows, dtype=jnp.int32)
    lagged_list = []
    for slot in range(DELAYS):
        offset = delays[slot]
        target_runs = lax.dynamic_slice_in_dim(runs_pad, first + offset, t_rows)
        valid = (positions + offset < total_rows) & (target_runs == own_runs)
        moved = lax.dynamic_slice_in_dim(extended, offset, t_rows, 0)
        lagged_list.append(jnp.where(valid[:, None], moved, jnp.zeros_like(moved)))
    stacked = jnp.stack(lagged_list, 1).reshape(t_rows, DELAYS * v_cols)
    cross = contract_rows(hidden, stacked)
    partial_cov = cross.reshape(d_local * DELAYS, v_cols).astype(jnp.bfloat16)
    panel_rows = lax.all_gather(panel, "tm", axis=0, tiled=True)
    rotated_part = contract_rows(
        lax.all_gather(panel_rows, "voxel", axis=1, tiled=True), partial_cov
    )
    rotated = lax.psum(rotated_part.astype(jnp.bfloat16), ("feature", "tm")).astype(jnp.float32)
    penalty = 2.0 ** ((ridge_grid.astype(jnp.float32) - 8.0) * 0.5)
    scaled = rotated[None] / (
        math.sqrt(total_rows) * (eigvals[None, :, None] + penalty[:, None, None])
    )
    return scaled.astype(jnp.bfloat16)


def solution(mesh):
    return jax.shard_map(
        shards,
        mesh=mesh,
        in_specs=(
            P("tm", "feature"),
            P("tm", "voxel"),
            P(("feature", "tm"), "voxel"),
            P(),
            P(),
            P(),
            P(),
        ),
        out_specs=P(None, None, "voxel"),
        check_vma=False,
    )
```

profile of v0, /device:TPU:2, one launch (start us, length us, event | category | flops | bytes accessed | tf_op | source)
XLA Modules:
  0.0 209.7 jit_solution(480760499588680285)
XLA Ops:
  6.5 14.4 %all_gather.6 = bf16[16384,4]{0,1:T(4,128)(2,1)} all-gather(bf16[4096,4]{0,1:T(4,128)(2,1)} %param.9), channel_id=1, replica_groups=mesh['voxel'=32,'feature'=4,'tm'=4] {'tm'}, dimensions={0}, use_global_device_ids=true | all-gather | bytes 163840 | tf_op jit(solution)/shard_map/all_gather | solution.py:45
  20.9 0.7 slice.28
  21.8 1.3 collective-permute-start
  23.1 1.6 fusion.49
  29.6 4.1 %fusion.48 = (pred[768]{0:T(1024)(128)(4,1)S(1)}, pred[768]{0:T(1024)(128)(4,1)S(1)}, pred[768]{0:T(1024)(128)(4,1)S(1)}, pred[768]{0:T(1024)(128)(4,1)S(1)}, pred[768]{0:T(1024)(128)(4,1)S(1)}) fusion(s32[]{:T(128)S(6)} %select_n.98, s32[3072]{0:T(1024)} %param.13, s32[]{:T(128)} %bitcast.14, s32[]{:T(128)S(6)} %mul.17, s32[]{:T(128)S(6)} %select_n.77, ...), kind=kLoop, calls=%fused_computation.77 | loop fusion | flops 16128 | bytes 22812 | tf_op jit(solution)/shard_map/and | solution.py:39
  33.7 0.7 multiply_power_fusion
  34.4 0.7 add_multiply_fusion
  35.1 2.7 %fusion.47 = (pred[768]{0:T(1024)(128)(4,1)S(1)}, pred[768]{0:T(1024)(128)(4,1)S(1)}, pred[768]{0:T(1024)(128)(4,1)S(1)}) fusion(s32[]{:T(128)S(6)} %select_n.95, s32[3072]{0:T(1024)} %param.13, s32[]{:T(128)} %bitcast.12, s32[]{:T(128)S(6)} %mul.17, s32[]{:T(128)S(6)} %select_n.77, s32[]{:T(128)S(6)} %select_n.80, s32[]{:T(128)} %bitcast.2, ...), kind=kLoop, calls=%fused_computation.76 | loop fusion | flops 9984 | bytes 20244 | tf_op jit(solution)/shard_map/and | solution.py:39
  38.5 1.1 copy.14
  53.9 0.2 fusion.12
  54.1 0.2 fusion.16
  54.3 0.2 fusion.20
  54.5 0.2 fusion.24
  54.7 0.2 fusion.28
  54.9 0.2 fusion.32
  55.1 0.2 fusion.4
  55.3 5.0 %convert_bitcast_fusion = bf16[2048,1024]{0,1:T(8,128)(2,1)} fusion(bf16[768,1024]{0,1:T(8,128)(2,1)S(1)} %bitcast.53, bf16[768,2048]{1,0:T(8,128)(2,1)S(1)} %copy-done), kind=kOutput, calls=%fused_computation | convolution fusion | flops 3223322624 | bytes 8912896 | tf_op jit(solution)/shard_map/dot_general | solution.py:19
  60.3 6.4 %copy.15 = bf16[2048,1024]{1,0:T(8,128)(2,1)} copy(bf16[2048,1024]{0,1:T(8,128)(2,1)} %convert_bitcast_fusion) | data formatting | bytes 8388608 | tf_op jit(solution)/shard_map/convert_element_type | solution.py:44
  66.7 7.4 %convert_element_type.26 = bf16[16384,128]{1,0:T(8,128)(2,1)} reshape(bf16[2048,1024]{1,0:T(8,128)(2,1)} %copy.15) | data formatting | bytes 8388608 | tf_op jit(solution)/shard_map/convert_element_type | solution.py:44
  74.1 17.7 %all-gather.3.cloned.1.call-done = bf16[32,4,16384]{2,1,0:T(4,128)(2,1)} async-done(((bf16[1,4,16384]{2,1,0:T(4,128)(2,1)}), bf16[32,4,16384]{2,1,0:T(4,128)(2,1)}) %all-gather.3.cloned.1.call-update) | async-done | bytes 4194320 | tf_op jit(solution)/shard_map/all_gather | solution.py:47
  91.8 6.9 %reshape.50 = bf16[128,16384]{1,0:T(8,128)(2,1)} reshape(bf16[32,4,16384]{2,1,0:T(4,128)(2,1)} %all-gather.3.cloned.1.call-done) | data formatting | bytes 8388608
  98.7 4.8 %fusion = bf16[128,128]{0,1:T(8,128)(2,1)S(1)} fusion(bf16[16384,128]{1,0:T(8,128)(2,1)} %convert_element_type.26, bf16[128,16384]{1,0:T(8,128)(2,1)} %reshape.50), kind=kOutput, calls=%fused_computation.3 | convolution fusion | flops 536887296 | bytes 8421376 | tf_op jit(solution)/shard_map/dot_general | solution.py:19
  103.5 97.9 %psum.7 = bf16[128,128]{0,1:T(8,128)(2,1)S(1)} all-reduce(bf16[128,128]{0,1:T(8,128)(2,1)S(1)} %fusion), channel_id=1, replica_groups=mesh['voxel'=32,'feature'=4,'tm'=4] {'feature','tm'}, use_global_device_ids=true, to_apply=%region_0.1 | all-reduce | flops 16384 | bytes 65536 | tf_op jit(solution)/shard_map/psum | solution.py:49
  201.5 1.4 divide_convert_fusion
  (8 shorter events, 0.5 us)
Async XLA Ops:
  6.5 48.8 %copy-start = (bf16[768,2048]{1,0:T(8,128)(2,1)S(1)}, bf16[768,2048]{1,0:T(8,128)(2,1)}, u32[]{:S(2)}) copy-start(bf16[768,2048]{1,0:T(8,128)(2,1)} %param.7) | copy-start | bytes 9437188
  6.5 85.3 %all-gather.3.cloned.1.call-start = ((), (), s32[]{:S(2)}) async-start(), calls=%async_computation | async-start | bytes 4325376 | tf_op jit(solution)/shard_map/all_gather | solution.py:47
  21.8 31.9 %collective-permute-start = (bf16[12,128]{0,1:T(8,128)(2,1)S(1)}, bf16[12,128]{0,1:T(8,128)(2,1)S(1)}, u32[]{:S(2)}, u32[]{:S(2)}) collective-permute-start(bf16[12,128]{0,1:T(8,128)(2,1)S(1)} %copy.13), channel_id=1, source_target_pairs={{1,0},{2,1},{3,2},{5,4},{6,5},{7,6},{9,8},{10,9},{11,10},{13,12},{... | collective-permute-start | bytes 9224 | tf_op jit(solution)/shard_map/ppermute | solution.py:15
Sparse Core Ops, SparseCore 0:
  21.1 70.7 all-gather.2
where the time goes:
time: 211 us; the launch traced here: 210 us
  blocking collectives  112 us (53%)
  between operations  33.1 us (16%)
  local copies, waits for them, and re-layouts  24.3 us (12%)
  waiting for transfers between devices  17.7 us (8%)
  other arithmetic  11.2 us (5%)
  matrix products  9.75 us (5%)
    psum x1, blocking collectives, shards(): lax.psum(rotated_part.astype(jnp.bfloat16), ('feature', 'tm'))  97.9 us
    all_gather x1, waiting for transfers between devices, shards(): lax.all_gather(panel_rows, 'voxel', axis=1, tiled=True)  17.7 us
    all_gather x1, blocking collectives, shards(): panel_rows = lax.all_gather(panel, 'tm', axis=0, tiled=True)  14.4 us
    convert_element_type x2, local copies, waits for them, and re-layouts, shards(): partial_cov = cross.reshape(d_local * DELAYS, v_cols).astype(jnp.bfloat16)  13.8 us
    dot_general x2, matrix products, contract_rows(): lax.dot_general(left, right, (((0,), (0,)), ((), ())), preferred_element_...  9.75 us
    unnamed x4, local copies, waits for them, and re-layouts  7.98 us
    and x2, other arithmetic, shards(): valid = (positions + offset < total_rows) & (target_runs == own_runs)  6.84 us
  transfers between devices with their start and end apart: 2, of which 1 were waited for; matrix products, arithmetic and copies ran while one was open for 15% of the time, Pallas kernels for 0%

commit v1 on v0

v1 whole, which is shorter than its diff:
```python
import functools
import math

import jax
import jax.numpy as jnp
from jax import lax
from jax.experimental import pallas as pl
from jax.experimental.pallas import tpu as pltpu
from jax.sharding import PartitionSpec as P

DELAYS = 8
MAXD = 12
LANES = 128
BF16 = jnp.bfloat16
F32 = jnp.float32


def iota(shape, dim):
    return lax.broadcasted_iota(jnp.int32, shape, dim)


def dot(left, right, dims=((1,), (0,))):
    return lax.dot_general(left, right, (dims, ((), ())), preferred_element_type=F32)


def kernel(
    sizes,
    delays_ref, ridge_ref, hidden_ref, bold_ref, panel_ref, eig_ref, runs_ref,
    out_ref,
    hid, bext, wbuf, pbuf, abuf, xbuf, rbuf, fbuf, masks,
    hid_sem, bold_sem, halo_sem, w_sem, a_sem, x_sem, r_sem, f_sem,
):
    n_v, n_f, n_t, t_rows, d_local, p_local = sizes
    d_chunk = d_local // n_t
    ext = t_rows + LANES
    n_c = ext // LANES
    i = lax.axis_index("voxel")
    f = lax.axis_index("feature")
    j = lax.axis_index("tm")

    hid_copies = [
        pltpu.make_async_copy(
            hidden_ref.at[:, pl.ds(c * d_chunk, d_chunk)], hid.at[c], hid_sem.at[c]
        )
        for c in range(n_t)
    ]
    bold_copy = pltpu.make_async_copy(bold_ref, bext.at[pl.ds(0, t_rows)], bold_sem)
    for copy in hid_copies:
        copy.start()
    bold_copy.start()
    bext[pl.ds(t_rows, LANES), :] = jnp.zeros((LANES, bext.shape[1]), BF16)

    def others(count, me, use):
        def body(step, carry):
            use(step, lax.rem(me + step, count))
            return carry
        lax.fori_loop(1, count, body, 0)

    barrier = pltpu.get_barrier_semaphore()

    def greet(axis):
        def use(step, peer):
            pl.semaphore_signal(
                barrier, inc=1, device_id={axis: peer}, device_id_type=pl.DeviceIdType.MESH
            )
        return use

    others(n_t, j, greet("tm"))
    others(n_f, f, greet("feature"))
    others(n_v, i, greet("voxel"))

    rows_local = panel_ref.shape[1]
    n_rows = DELAYS * p_local
    spread = (iota((n_rows, p_local), 0) % p_local == iota((n_rows, p_local), 1)).astype(BF16)
    tall = dot(spread, panel_ref[...])
    keep = iota(tall.shape, 1) % DELAYS == iota(tall.shape, 0) // p_local
    tall = jnp.where(keep, tall, 0.0).astype(BF16)
    block = DELAYS * LANES
    squeeze = (iota((block, LANES), 0) // DELAYS == iota((block, LANES), 1)).astype(BF16)
    for b in range(rows_local // block):
        part = dot(tall[:, b * block:(b + 1) * block], squeeze)
        wbuf[j, :, pl.ds(b * LANES, LANES)] = part.astype(BF16)

    pl.semaphore_wait(barrier, n_t + n_f + n_v - 3)

    def send(src, dst, sems, slot, axis, peer):
        return pltpu.make_async_remote_copy(
            src_ref=src, dst_ref=dst, send_sem=sems.at[0, slot], recv_sem=sems.at[1, slot],
            device_id={axis: peer}, device_id_type=pl.DeviceIdType.MESH,
        )

    before = lax.rem(j + n_t - 1, n_t)
    halo = pltpu.make_async_remote_copy(
        src_ref=bold_ref.at[pl.ds(0, 16)], dst_ref=bext.at[pl.ds(t_rows, 16)],
        send_sem=halo_sem.at[0], recv_sem=halo_sem.at[1],
        device_id={"tm": before}, device_id_type=pl.DeviceIdType.MESH,
    )
    w_sends = [
        send(wbuf.at[j], wbuf.at[j], w_sem, s - 1, "tm", lax.rem(j + s, n_t)) for s in range(1, n_t)
    ]
    for copy in w_sends:
        copy.start()
    halo.start()

    own_runs = runs_ref[:, pl.ds(pl.multiple_of(j * t_rows, LANES), t_rows)]
    next_runs = runs_ref[:, pl.ds(pl.multiple_of(lax.rem(j + 1, n_t) * t_rows, LANES), LANES)]
    runs = jnp.broadcast_to(jnp.concatenate([own_runs, next_runs], 1), (8, ext))
    end = jnp.where(j == n_t - 1, t_rows, ext)
    inside = iota((8, ext), 1) < end
    for m in range(1, MAXD + 1):
        same = (pltpu.roll(runs, m, 1) == runs) & inside
        masks[m - 1] = jnp.where(same, 1.0, 0.0)
    shape = (8 * MAXD, n_rows)
    lag = iota(shape, 0) // 8 + 1
    delay_of = iota(shape, 1) // p_local
    right_p = iota(shape, 0) % 8 == iota(shape, 1) % p_local
    wanted = jnp.zeros(shape, jnp.int32)
    for k in range(DELAYS):
        wanted = jnp.where(delay_of == k, delays_ref[k], wanted)
    pick = jnp.where(right_p & (wanted == lag), 1.0, 0.0).astype(BF16)
    pick = jnp.concatenate([pick, pick], 1)
    n_x = n_v * 8
    order = (
        (iota((n_x, n_x), 0) % n_v == iota((n_x, n_x), 1) // 8)
        & (iota((n_x, n_x), 0) // n_v == iota((n_x, n_x), 1) % 8)
    ).astype(BF16)

    for copy in hid_copies:
        copy.wait()
    nt = ((1,), (1,))
    g = dot(wbuf[j], hid[j], nt)
    for s in range(1, n_t):
        w_sends[s - 1].wait_recv()
        source = lax.rem(j + n_t - s, n_t)
        g = g + dot(wbuf[source], hid[source], nt)

    high = g.astype(BF16)
    low = (g - high.astype(F32)).astype(BF16)
    lagged = dot(pick, jnp.concatenate([high, low], 0))
    lagged = jnp.concatenate([lagged, jnp.zeros((8 * MAXD, LANES), F32)], 1)
    gs = jnp.zeros((8, ext), F32)
    for m in range(1, MAXD + 1):
        gs = gs + pltpu.roll(lagged[8 * (m - 1):8 * m], m, 1) * masks[m - 1]

    row = iota((8, LANES), 0)
    for p in range(p_local):
        tile = jnp.zeros((8, LANES), F32)
        for c in range(n_c):
            line = jnp.broadcast_to(gs[p:p + 1, c * LANES:(c + 1) * LANES], (8, LANES))
            tile = jnp.where(row == c, line, tile)
        pbuf[p] = tile.astype(BF16)
    abuf[f] = pbuf[f]
    a_sends = [
        send(pbuf.at[lax.rem(f + s, n_f)], abuf.at[f], a_sem, s - 1, "feature", lax.rem(f + s, n_f))
        for s in range(1, n_f)
    ]
    for copy in a_sends:
        copy.start()
    for copy in a_sends:
        copy.wait_recv()
    total = abuf[0].astype(F32)
    for s in range(1, n_f):
        total = total + abuf[s].astype(F32)
    xbuf[i] = total.astype(BF16)

    def x_send(step, peer):
        pltpu.make_async_remote_copy(
            src_ref=xbuf.at[i], dst_ref=xbuf.at[i], send_sem=x_sem.at[0], recv_sem=x_sem.at[1],
            device_id={"voxel": peer}, device_id_type=pl.DeviceIdType.MESH,
        ).start()

    others(n_v, i, x_send)
    halo.wait_recv()
    bold_copy.wait()
    arrived = xbuf.at[pl.ds(0, n_v - 1)]
    pltpu.make_async_copy(arrived, arrived, x_sem.at[1]).wait()

    x = dot(order, xbuf[...].reshape(n_x, LANES)).astype(BF16)
    r = jnp.zeros((n_v, bext.shape[1]), F32)
    for c in range(n_c):
        r = r + dot(x[c * n_v:(c + 1) * n_v], bext[pl.ds(c * LANES, LANES), :])
    rbuf[j] = r.astype(BF16)
    r_sends = [
        send(rbuf.at[j], rbuf.at[j], r_sem, s - 1, "tm", lax.rem(j + s, n_t)) for s in range(1, n_t)
    ]
    for copy in r_sends:
        copy.start()
    for copy in r_sends:
        copy.wait_recv()
    r = rbuf[0].astype(F32)
    for s in range(1, n_t):
        r = r + rbuf[s].astype(F32)

    fbuf[f] = r.astype(BF16)
    f_sends = [
        send(fbuf.at[f], fbuf.at[f], f_sem, s - 1, "feature", lax.rem(f + s, n_f))
        for s in range(1, n_f)
    ]
    for copy in f_sends:
        copy.start()
    for copy in f_sends:
        copy.wait_recv()
    for s in range(n_f):
        out_ref[pl.ds(s, n_v, stride=n_f), :] = fbuf[s].astype(F32)

    for copy in w_sends + a_sends + r_sends + f_sends + [halo]:
        copy.wait_send()
    pltpu.make_async_copy(arrived, arrived, x_sem.at[0]).wait()


def shards(hidden, bold, panel, eigvals, ridge_grid, delays, runs):
    n_v, n_f, n_t = (lax.axis_size(axis) for axis in ("voxel", "feature", "tm"))
    t_rows, d_local = hidden.shape
    v_cols = bold.shape[1]
    p_local = panel.shape[1]
    n_p = n_v * p_local
    assert p_local == n_f and n_v * 8 % 16 == 0
    ext = t_rows + LANES
    d_chunk = d_local // n_t
    vmem = pl.BlockSpec(memory_space=pltpu.VMEM)
    smem = pl.BlockSpec(memory_space=pltpu.SMEM)
    hbm = pl.BlockSpec(memory_space=pl.ANY)
    dma = pltpu.SemaphoreType.DMA
    rotated = pl.pallas_call(
        functools.partial(kernel, (n_v, n_f, n_t, t_rows, d_local, p_local)),
        out_shape=jax.ShapeDtypeStruct((n_p, v_cols), F32),
        in_specs=[smem, smem, hbm, hbm, vmem, vmem, vmem],
        out_specs=vmem,
        scratch_shapes=[
            pltpu.VMEM((n_t, t_rows, d_chunk), BF16),
            pltpu.VMEM((ext, v_cols), BF16),
            pltpu.VMEM((n_t, DELAYS * p_local, d_chunk), BF16),
            pltpu.VMEM((p_local, 8, LANES), BF16),
            pltpu.VMEM((n_f, 8, LANES), BF16),
            pltpu.VMEM((n_v, 8, LANES), BF16),
            pltpu.VMEM((n_t, n_v, v_cols), BF16),
            pltpu.VMEM((n_f, n_v, v_cols), BF16),
            pltpu.VMEM((MAXD, 8, ext), F32),
            dma((n_t,)),
            dma,
            dma((2,)),
            dma((2, n_t - 1)),
            dma((2, n_f - 1)),
            dma((2,)),
            dma((2, n_t - 1)),
            dma((2, n_f - 1)),
        ],
        compiler_params=pltpu.CompilerParams(collective_id=0, has_side_effects=True),
        name="sweep",
    )(delays, ridge_grid, hidden, bold, panel.T, eigvals[None], runs[None])
    penalty = 2.0 ** ((ridge_grid.astype(F32) - 8.0) * 0.5)
    scaled = rotated[None] / (
        math.sqrt(t_rows * n_t) * (eigvals[None, :, None] + penalty[:, None, None])
    )
    return scaled.astype(BF16)


def solution(mesh):
    return jax.shard_map(
        shards,
        mesh=mesh,
        in_specs=(
            P("tm", "feature"),
            P("tm", "voxel"),
            P(("feature", "tm"), "voxel"),
            P(),
            P(),
            P(),
            P(),
        ),
        out_specs=P(None, None, "voxel"),
        check_vma=False,
    )
```

time: 211 us -> 49.2 us (0.23)
  the two profiles are of different devices: /device:TPU:2 before, /device:TPU:1 now
where the time goes in v1:
time: 49.2 us; the launch traced here: 49 us
  Pallas kernels  45.4 us (92%)
  other arithmetic  3.59 us (7%)
    pallas_call x1, Pallas kernels, shards(): pl.pallas_call(functools.partial(kernel, (n_v, n_f, n_t, t_rows, d_local,...  45.4 us
    convert_element_type x1, other arithmetic, shards(): return scaled.astype(BF16)  2.2 us

profile of v1, /device:TPU:1, one launch (start us, length us, event | category | flops | bytes accessed | tf_op | source)
XLA Modules:
  0.0 49.0 jit_solution(7297519182353649629)
XLA Ops:
  0.0 0.7 %multiply_power_fusion = f32[24]{0:T(128)S(1)} fusion(s32[24]{0:T(128)} %ridge_ref.1), kind=kLoop, calls=%fused_computation.2 | loop fusion | flops 72 | bytes 192 | tf_op jit(solution)/shard_map/pow | solution.py:251
  0.7 0.7 %add_multiply_fusion = f32[24,128]{1,0:T(8,128)S(1)} fusion(f32[24]{0:T(128)S(1)} %multiply_power_fusion, f32[128]{0:T(128)} %param.10), kind=kLoop, calls=%fused_computation.1 | loop fusion | flops 6144 | bytes 12896 | tf_op jit(solution)/shard_map/mul | solution.py:253
  1.4 45.4 %sweep.1 = f32[128,128]{1,0:T(8,128)} custom-call(s32[8]{0:T(128)} %delays_ref.1, s32[24]{0:T(128)} %ridge_ref.1, bf16[768,2048]{1,0:T(8,128)(2,1)} %hidden_ref.1, bf16[768,128]{1,0:T(8,128)(2,1)} %bold_ref.1, bf16[4,4096]{1,0:T(4,128)(2,1)} %bitcast.3, f32[1,128]{1,0:T(1,128)} %bitcast.5, s32[1,3072]{1,0:T(1,128)} %bitcast.4), custom_call_target="tpu_custom_call" | custom-call | tf_op jit(solution)/shard_map/sweep/pallas_call | solution.py:224
  46.8 2.2 %divide_convert_fusion = bf16[24,128,128]{2,1,0:T(8,128)(2,1)} fusion(f32[24,128]{1,0:T(8,128)S(1)} %add_multiply_fusion, f32[128,128]{1,0:T(8,128)} %sweep.1), kind=kLoop, calls=%fused_computation | loop fusion | flops 786432 | bytes 864256 | tf_op jit(solution)/shard_map/convert_element_type | solution.py:255

commit v2 on v1

v2 whole, which is shorter than its diff:
```python
import functools
import math

import jax
import jax.numpy as jnp
from jax import lax
from jax.experimental import pallas as pl
from jax.experimental.pallas import tpu as pltpu
from jax.sharding import PartitionSpec as P

DELAYS = 8
MAXD = 12
LANES = 128
HALF = 512
N_ZLO = 4
BF16 = jnp.bfloat16
F32 = jnp.float32
MESH = pl.DeviceIdType.MESH


def iota(shape, dim):
    return lax.broadcasted_iota(jnp.int32, shape, dim)


def dot(left, right, dims=((1,), (0,))):
    return lax.dot_general(left, right, (dims, ((), ())), preferred_element_type=F32)


def kernel(
    sizes,
    delays_hbm, hidden_ref, bold_ref, panel_hbm, runs_hbm,
    out_ref,
    delays_ref, panel_ref, runs_ref,
    hid, bext, wbuf, abuf, xbuf, sbuf, rbuf, masks,
    in_sem, hid_sem, bold_sem, halo_sem, w_sem, a_sem, x_sem, r_sem, near_sem, far_sem,
):
    n_v, n_f, n_t, t_rows, d_local, p_local = sizes
    d_chunk = d_local // n_t
    ext = t_rows + LANES
    n_z = n_f * N_ZLO
    n_x = n_v // (2 * N_ZLO)
    i = lax.axis_index("voxel")
    f = lax.axis_index("feature")
    j = lax.axis_index("tm")
    core = lax.rem(i, 2)
    x = i // (2 * N_ZLO)
    z = f * N_ZLO + lax.rem(i // 2, N_ZLO)
    chip = i // 2

    def at(dx=0, dz=0, dj=0, flip=False):
        xx = lax.rem(x + dx, n_x)
        zz = lax.rem(z + dz + n_z, n_z)
        cc = 1 - core if flip else core
        return {
            "voxel": (xx * N_ZLO + lax.rem(zz, N_ZLO)) * 2 + cc,
            "feature": zz // N_ZLO,
            "tm": lax.rem(j + dj, n_t),
        }

    def signal(sem, where):
        pl.semaphore_signal(sem, inc=1, device_id=where, device_id_type=MESH)

    barrier = pltpu.get_barrier_semaphore()
    near = [at(dj=s, flip=w) for s in range(n_t) for w in (False, True) if s or w]
    near += [at(dx=s) for s in range(1, n_x)]
    along = [at(dz=s) for s in (-2, -1, 1, 2)]
    for where in near + along:
        signal(barrier, where)

    panel_copy = pltpu.make_async_copy(panel_hbm, panel_ref, in_sem.at[0])
    runs_copy = pltpu.make_async_copy(runs_hbm, runs_ref, in_sem.at[1])
    delays_copy = pltpu.make_async_copy(delays_hbm, delays_ref, in_sem.at[2])
    panel_copy.start()
    runs_copy.start()
    delays_copy.start()
    hid_copies = [
        pltpu.make_async_copy(
            hidden_ref.at[:, pl.ds(c * d_chunk, d_chunk)], hid.at[c], hid_sem.at[c]
        )
        for c in range(n_t)
    ]
    for copy in hid_copies:
        copy.start()
    bold_copy = pltpu.make_async_copy(bold_ref, bext.at[core, pl.ds(0, t_rows)], bold_sem.at[0])
    bold_copy.start()

    rows_local = panel_ref.shape[1]
    n_rows = DELAYS * p_local
    block = DELAYS * LANES
    spread = (iota((n_rows, p_local), 0) % p_local == iota((n_rows, p_local), 1)).astype(BF16)
    squeeze = (iota((block, LANES), 0) // DELAYS == iota((block, LANES), 1)).astype(BF16)
    keep = iota((n_rows, rows_local), 1) % DELAYS == iota((n_rows, rows_local), 0) // p_local
    panel_copy.wait()
    tall = dot(spread, panel_ref[...])
    tall = jnp.where(keep, tall, 0.0).astype(BF16)
    for b in range(rows_local // block):
        part = dot(tall[:, b * block:(b + 1) * block], squeeze)
        wbuf[j, :, pl.ds(b * LANES, LANES)] = part.astype(BF16)

    pl.semaphore_wait(barrier, len(near) + len(along))

    def remote(src, dst, sems, slot, where):
        return pltpu.make_async_remote_copy(
            src_ref=src, dst_ref=dst, send_sem=sems.at[0, slot], recv_sem=sems.at[1, slot],
            device_id=where, device_id_type=MESH,
        )

    w_sends = [remote(wbuf.at[j], wbuf.at[j], w_sem, s - 1, at(dj=s)) for s in range(1, n_t)]
    for copy in w_sends:
        copy.start()
    for where in along:
        signal(near_sem, where)
    tail = HALF * 2 - t_rows - 16
    for c in range(2):
        bext[c, pl.ds(t_rows + 16, tail), :] = jnp.zeros((tail, LANES), BF16)
    halos = [
        remote(
            bold_ref.at[pl.ds(0, 16)], bext.at[core, pl.ds(t_rows, 16)],
            halo_sem, s, at(dj=n_t - 1, flip=s == 1),
        )
        for s in range(2)
    ]
    share = pltpu.make_async_remote_copy(
        src_ref=bold_ref, dst_ref=bext.at[core, pl.ds(0, t_rows)],
        send_sem=bold_sem.at[1], recv_sem=bold_sem.at[2],
        device_id=at(flip=True), device_id_type=MESH,
    )
    for copy in halos + [share]:
        copy.start()

    runs_copy.wait()
    own_runs = runs_ref[:, pl.ds(pl.multiple_of(j * t_rows, LANES), t_rows)]
    next_runs = runs_ref[:, pl.ds(pl.multiple_of(lax.rem(j + 1, n_t) * t_rows, LANES), LANES)]
    runs = jnp.broadcast_to(jnp.concatenate([own_runs, next_runs], 1), (8, ext))
    end = jnp.where(j == n_t - 1, t_rows, ext)
    inside = iota((8, ext), 1) < end
    for m in range(1, MAXD + 1):
        same = (pltpu.roll(runs, m, 1) == runs) & inside
        masks[m - 1] = jnp.where(same, 1.0, 0.0)

    pl.semaphore_wait(near_sem, len(along))
    for where in (at(dz=-4), at(dz=4)):
        signal(far_sem, where)

    delays_copy.wait()
    shape = (8 * MAXD, n_rows)
    lag = iota(shape, 0) // 8 + 1
    delay_of = iota(shape, 1) // p_local
    right_p = iota(shape, 0) % p_local == iota(shape, 1) % p_local
    wanted = jnp.zeros(shape, jnp.int32)
    for k in range(DELAYS):
        wanted = jnp.where(delay_of == k, delays_ref[k], wanted)
    pick = jnp.where(right_p & (wanted == lag), 1.0, 0.0).astype(BF16)
    pick = jnp.concatenate([pick, pick], 1)

    for copy in hid_copies:
        copy.wait()
    nt = ((1,), (1,))
    g = dot(wbuf[j], hid[j], nt)
    for s in (1, 3, 2):
        w_sends[s - 1].wait_recv()
        source = lax.rem(j + n_t - s, n_t)
        g = g + dot(wbuf[source], hid[source], nt)

    high = g.astype(BF16)
    low = (g - high.astype(F32)).astype(BF16)
    lagged = dot(pick, jnp.concatenate([high, low], 0))
    lagged = jnp.concatenate([lagged, jnp.zeros((8 * MAXD, LANES), F32)], 1)
    gs = jnp.zeros((8, ext), F32)
    for m in range(1, MAXD + 1):
        gs = gs + pltpu.roll(lagged[8 * (m - 1):8 * m], m, 1) * masks[m - 1]

    second = jnp.concatenate([gs[:, HALF:], jnp.zeros((8, 2 * HALF - ext), F32)], 1)
    low_rows = iota((8, HALF), 0) < p_local
    abuf[f] = jnp.where(low_rows, gs[:, :HALF], second).astype(BF16)
    pl.semaphore_wait(far_sem, 2)
    a_sends = [remote(abuf.at[f], abuf.at[f], a_sem, s - 1, at(dz=N_ZLO * s)) for s in (2, 1, 3)]
    for copy in a_sends:
        copy.start()
    for copy in a_sends:
        copy.wait_recv()
    total = abuf[0].astype(F32)
    for s in range(1, n_f):
        total = total + abuf[s].astype(F32)
    xbuf[chip] = total.astype(BF16)

    steps = [(dx, dz) for dx in (2, 1, 3, 0) for dz in (-2, -1, 1, 0) if dx or dz]
    for dx, dz in steps:
        pltpu.make_async_remote_copy(
            src_ref=xbuf.at[chip], dst_ref=xbuf.at[chip],
            send_sem=x_sem.at[0], recv_sem=x_sem.at[1],
            device_id=at(dx=dx, dz=dz), device_id_type=MESH,
        ).start()
    for copy in halos + [share]:
        copy.wait_recv()
    bold_copy.wait()
    arrived = xbuf.at[pl.ds(0, n_v // 2 - 1)]
    pltpu.make_async_copy(arrived, arrived, x_sem.at[1]).wait()

    sums = xbuf[...].reshape(n_v // 2 * 8, HALF)
    halves = []
    for h in range(2):
        both = jnp.concatenate([bext[c, pl.ds(h * HALF, HALF), :] for c in range(2)], 1)
        halves.append(dot(sums, both))
    upper = iota((8, 2 * LANES), 0) < p_local
    for g2 in range(n_v // 4):
        a, b = slice(16 * g2, 16 * g2 + 8), slice(16 * g2 + 8, 16 * g2 + 16)
        u = jnp.where(upper, halves[0][a], halves[1][b])
        w = jnp.where(upper, halves[0][b], halves[1][a])
        r = (u + pltpu.roll(w, 4, 0)).astype(BF16)
        for c in range(2):
            sbuf[c, pl.ds(8 * g2, 8), :] = r[:, c * LANES:(c + 1) * LANES]
    rbuf[j, core] = sbuf[core]
    r_sends = []
    for n, (s, w) in enumerate(((2, True), (2, False), (1, True), (3, True), (1, False), (3, False), (0, True))):
        r_sends.append(
            remote(sbuf.at[1 - core if w else core], rbuf.at[j, core], r_sem, n, at(dj=s, flip=w))
        )
    for copy in r_sends:
        copy.start()
    for copy in r_sends:
        copy.wait_recv()
    upper = iota((8, LANES), 0) < p_local
    parts = []
    for c in range(2):
        r = rbuf[0, c].astype(F32)
        for s in range(1, n_t):
            r = r + rbuf[s, c].astype(F32)
        parts.append(r)
    for g2 in range(n_v // 4):
        v0, v1 = parts[0][8 * g2:8 * g2 + 8], parts[1][8 * g2:8 * g2 + 8]
        out_ref[pl.ds(16 * g2, 8), :] = jnp.where(upper, v0, pltpu.roll(v1, 4, 0))
        out_ref[pl.ds(16 * g2 + 8, 8), :] = jnp.where(upper, pltpu.roll(v0, 4, 0), v1)

    for copy in w_sends + a_sends + r_sends + halos + [share]:
        copy.wait_send()
    pltpu.make_async_copy(arrived, arrived, x_sem.at[0]).wait()


def shards(hidden, bold, panel, eigvals, ridge_grid, delays, runs):
    n_v, n_f, n_t = (lax.axis_size(axis) for axis in ("voxel", "feature", "tm"))
    t_rows, d_local = hidden.shape
    v_cols = bold.shape[1]
    p_local = panel.shape[1]
    n_p = n_v * p_local
    ext = t_rows + LANES
    d_chunk = d_local // n_t
    vmem = pl.BlockSpec(memory_space=pltpu.VMEM)
    hbm = pl.BlockSpec(memory_space=pl.ANY)
    dma = pltpu.SemaphoreType.DMA
    rotated = pl.pallas_call(
        functools.partial(kernel, (n_v, n_f, n_t, t_rows, d_local, p_local)),
        out_shape=jax.ShapeDtypeStruct((n_p, v_cols), F32),
        in_specs=[hbm] * 5,
        out_specs=vmem,
        scratch_shapes=[
            pltpu.SMEM((DELAYS,), jnp.int32),
            pltpu.VMEM((p_local, panel.shape[0]), BF16),
            pltpu.VMEM((1, runs.shape[0]), jnp.int32),
            pltpu.VMEM((n_t, t_rows, d_chunk), BF16),
            pltpu.VMEM((2, 2 * HALF, v_cols), BF16),
            pltpu.VMEM((n_t, DELAYS * p_local, d_chunk), BF16),
            pltpu.VMEM((n_f, 8, HALF), BF16),
            pltpu.VMEM((n_v // 2, 8, HALF), BF16),
            pltpu.VMEM((2, n_v * 2, v_cols), BF16),
            pltpu.VMEM((n_t, 2, n_v * 2, v_cols), BF16),
            pltpu.VMEM((MAXD, 8, ext), F32),
            dma((3,)),
            dma((n_t,)),
            dma((3,)),
            dma((2, 2)),
            dma((2, n_t - 1)),
            dma((2, n_f - 1)),
            dma((2,)),
            dma((2, 2 * n_t - 1)),
            pltpu.SemaphoreType.REGULAR,
            pltpu.SemaphoreType.REGULAR,
        ],
        compiler_params=pltpu.CompilerParams(collective_id=0, has_side_effects=True),
        name="sweep",
    )(delays, hidden, bold, panel.T, runs[None])
    penalty = 2.0 ** ((ridge_grid.astype(F32) - 8.0) * 0.5)
    scaled = rotated[None] / (
        math.sqrt(t_rows * n_t) * (eigvals[None, :, None] + penalty[:, None, None])
    )
    return scaled.astype(BF16)


def solution(mesh):
    return jax.shard_map(
        shards,
        mesh=mesh,
        in_specs=(
            P("tm", "feature"),
            P("tm", "voxel"),
            P(("feature", "tm"), "voxel"),
            P(),
            P(),
            P(),
            P(),
        ),
        out_specs=P(None, None, "voxel"),
        check_vma=False,
    )
```

time: 49.2 us -> 40.2 us (0.82)
  Pallas kernels: 45.4 us -> 36.4 us
    pallas_call x1, Pallas kernels: 45.4 us -> 36.4 us  [shards(): pl.pallas_call(functools.partial(kernel, (n_v, n_f, n_t, t_rows, d_local,...]
where the time goes in v2:
time: 40.2 us; the launch traced here: 40 us
  Pallas kernels  36.4 us (91%)
  other arithmetic  3.59 us (9%)
    pallas_call x1, Pallas kernels, shards(): pl.pallas_call(functools.partial(kernel, (n_v, n_f, n_t, t_rows, d_local,...  36.4 us
    convert_element_type x1, other arithmetic, shards(): return scaled.astype(BF16)  2.2 us

profile of v2, /device:TPU:1, one launch (start us, length us, event | category | flops | bytes accessed | tf_op | source)
XLA Modules:
  0.0 40.0 jit_solution(16534859281556622373)
XLA Ops:
  0.0 0.7 %multiply_power_fusion = f32[24]{0:T(128)S(1)} fusion(s32[24]{0:T(128)} %param.11), kind=kLoop, calls=%fused_computation.2 | loop fusion | flops 72 | bytes 192 | tf_op jit(solution)/shard_map/pow | solution.py:282
  0.7 0.7 %add_multiply_fusion = f32[24,128]{1,0:T(8,128)S(1)} fusion(f32[24]{0:T(128)S(1)} %multiply_power_fusion, f32[128]{0:T(128)} %param.10), kind=kLoop, calls=%fused_computation.1 | loop fusion | flops 6144 | bytes 12896 | tf_op jit(solution)/shard_map/mul | solution.py:284
  1.4 36.4 %sweep.1 = f32[128,128]{1,0:T(8,128)} custom-call(s32[8]{0:T(128)} %delays_hbm.1, bf16[768,2048]{1,0:T(8,128)(2,1)} %hidden_ref.1, bf16[768,128]{1,0:T(8,128)(2,1)} %bold_ref.1, bf16[4,4096]{1,0:T(4,128)(2,1)} %bitcast.2, s32[1,3072]{1,0:T(1,128)} %bitcast.3), custom_call_target="tpu_custom_call" | custom-call | tf_op jit(solution)/shard_map/sweep/pallas_call | solution.py:251
  37.8 2.2 %divide_convert_fusion = bf16[24,128,128]{2,1,0:T(8,128)(2,1)} fusion(f32[24,128]{1,0:T(8,128)S(1)} %add_multiply_fusion, f32[128,128]{1,0:T(8,128)} %sweep.1), kind=kLoop, calls=%fused_computation | loop fusion | flops 786432 | bytes 864256 | tf_op jit(solution)/shard_map/convert_element_type | solution.py:286

commit v3 on v2

--- a/solution.py
+++ b/solution.py
@@ -10,6 +10,7 @@
 
 DELAYS = 8
 MAXD = 12
+RIDGES = 24
 LANES = 128
 HALF = 512
 N_ZLO = 4
@@ -28,9 +29,9 @@
 
 def kernel(
     sizes,
-    delays_hbm, hidden_ref, bold_ref, panel_hbm, runs_hbm,
+    delays_hbm, ridge_hbm, hidden_ref, bold_ref, panel_hbm, runs_hbm, eig_hbm,
     out_ref,
-    delays_ref, panel_ref, runs_ref,
+    delays_ref, ridge_ref, panel_ref, runs_ref, eig_ref, scale,
     hid, bext, wbuf, abuf, xbuf, sbuf, rbuf, masks,
     in_sem, hid_sem, bold_sem, halo_sem, w_sem, a_sem, x_sem, r_sem, near_sem, far_sem,
 ):
@@ -73,6 +74,10 @@
     panel_copy.start()
     runs_copy.start()
     delays_copy.start()
+    ridge_copy = pltpu.make_async_copy(ridge_hbm, ridge_ref, in_sem.at[3])
+    eig_copy = pltpu.make_async_copy(eig_hbm, eig_ref, in_sem.at[4])
+    ridge_copy.start()
+    eig_copy.start()
     hid_copies = [
         pltpu.make_async_copy(
             hidden_ref.at[:, pl.ds(c * d_chunk, d_chunk)], hid.at[c], hid_sem.at[c]
@@ -177,6 +182,20 @@
     a_sends = [remote(abuf.at[f], abuf.at[f], a_sem, s - 1, at(dz=N_ZLO * s)) for s in (2, 1, 3)]
     for copy in a_sends:
         copy.start()
+
+    ridge_copy.wait()
+    eig_copy.wait()
+    n_p = eig_ref.shape[1]
+    eig = jnp.broadcast_to(eig_ref[...], (LANES, n_p)).T
+
+    def factor(n, carry):
+        level = jnp.full((8, LANES), ridge_ref[n], jnp.int32).astype(F32)
+        penalty = jnp.exp2((level - 8.0) * 0.5)
+        whole_penalty = jnp.concatenate([penalty] * (n_p // 8), 0)
+        scale[n] = 1.0 / (math.sqrt(t_rows * n_t) * (eig + whole_penalty))
+        return carry
+
+    lax.fori_loop(0, RIDGES, factor, 0)
     for copy in a_sends:
         copy.wait_recv()
     total = abuf[0].astype(F32)
@@ -227,10 +246,14 @@
         for s in range(1, n_t):
             r = r + rbuf[s, c].astype(F32)
         parts.append(r)
+    tiles = []
     for g2 in range(n_v // 4):
         v0, v1 = parts[0][8 * g2:8 * g2 + 8], parts[1][8 * g2:8 * g2 + 8]
-        out_ref[pl.ds(16 * g2, 8), :] = jnp.where(upper, v0, pltpu.roll(v1, 4, 0))
-        out_ref[pl.ds(16 * g2 + 8, 8), :] = jnp.where(upper, pltpu.roll(v0, 4, 0), v1)
+        tiles.append(jnp.where(upper, v0, pltpu.roll(v1, 4, 0)))
+        tiles.append(jnp.where(upper, pltpu.roll(v0, 4, 0), v1))
+    rotated = jnp.concatenate(tiles, 0)
+    for n in range(RIDGES):
+        out_ref[n] = (rotated * scale[n]).astype(BF16)
 
     for copy in w_sends + a_sends + r_sends + halos + [share]:
         copy.wait_send()
@@ -245,18 +268,20 @@
     n_p = n_v * p_local
     ext = t_rows + LANES
     d_chunk = d_local // n_t
-    vmem = pl.BlockSpec(memory_space=pltpu.VMEM)
     hbm = pl.BlockSpec(memory_space=pl.ANY)
     dma = pltpu.SemaphoreType.DMA
-    rotated = pl.pallas_call(
+    return pl.pallas_call(
         functools.partial(kernel, (n_v, n_f, n_t, t_rows, d_local, p_local)),
-        out_shape=jax.ShapeDtypeStruct((n_p, v_cols), F32),
-        in_specs=[hbm] * 5,
-        out_specs=vmem,
+        out_shape=pltpu.VMEM((RIDGES, n_p, v_cols), BF16),
+        in_specs=[hbm] * 7,
+        out_specs=pl.BlockSpec(memory_space=pltpu.VMEM),
         scratch_shapes=[
             pltpu.SMEM((DELAYS,), jnp.int32),
+            pltpu.SMEM((RIDGES,), jnp.int32),
             pltpu.VMEM((p_local, panel.shape[0]), BF16),
             pltpu.VMEM((1, runs.shape[0]), jnp.int32),
+            pltpu.VMEM((1, n_p), F32),
+            pltpu.VMEM((RIDGES, n_p, v_cols), F32),
             pltpu.VMEM((n_t, t_rows, d_chunk), BF16),
             pltpu.VMEM((2, 2 * HALF, v_cols), BF16),
             pltpu.VMEM((n_t, DELAYS * p_local, d_chunk), BF16),
@@ -265,7 +290,7 @@
             pltpu.VMEM((2, n_v * 2, v_cols), BF16),
             pltpu.VMEM((n_t, 2, n_v * 2, v_cols), BF16),
             pltpu.VMEM((MAXD, 8, ext), F32),
-            dma((3,)),
+            dma((5,)),
             dma((n_t,)),
             dma((3,)),
             dma((2, 2)),
@@ -278,12 +303,7 @@
         ],
         compiler_params=pltpu.CompilerParams(collective_id=0, has_side_effects=True),
         name="sweep",
-    )(delays, hidden, bold, panel.T, runs[None])
-    penalty = 2.0 ** ((ridge_grid.astype(F32) - 8.0) * 0.5)
-    scaled = rotated[None] / (
-        math.sqrt(t_rows * n_t) * (eigvals[None, :, None] + penalty[:, None, None])
-    )
-    return scaled.astype(BF16)
+    )(delays, ridge_grid, hidden, bold, panel.T, runs[None], eigvals[None])
 
 
 def solution(mesh):

time: 40.2 us -> 36.9 us (0.918)
  other arithmetic: 3.59 us -> 0 us
  local copies, waits for them, and re-layouts: 0 us -> 0.88 us
  Pallas kernels: 36.4 us -> 35.9 us
    convert_element_type x1 -> x0, other arithmetic: 2.2 us -> none  [shards(): return scaled.astype(BF16)]
    unnamed x0 -> x1, local copies, waits for them, and re-layouts: none -> 0.88 us
    mul x1 -> x0, other arithmetic: 0.73 us -> none  [shards(): math.sqrt(t_rows * n_t) * (eigvals[None, :, None] + penalty[:, None, None])]
    pow x1 -> x0, other arithmetic: 0.66 us -> none  [shards(): penalty = 2.0 ** ((ridge_grid.astype(F32) - 8.0) * 0.5)]
    pallas_call x1, Pallas kernels: 36.4 us -> 35.9 us  [shards(): pl.pallas_call(functools.partial(kernel, (n_v, n_f, n_t, t_rows, d_local,...]
where the time goes in v3:
time: 36.9 us; the launch traced here: 36.8 us
  Pallas kernels  35.9 us (97%)
  local copies, waits for them, and re-layouts  0.88 us (2%)
    pallas_call x1, Pallas kernels, shards(): pl.pallas_call(functools.partial(kernel, (n_v, n_f, n_t, t_rows, d_local,...  35.9 us
    unnamed x1, local copies, waits for them, and re-layouts  0.88 us

profile of v3, /device:TPU:1, one launch (start us, length us, event | category | flops | bytes accessed | tf_op | source)
XLA Modules:
  0.0 36.8 jit_solution(5031287180810754051)
XLA Ops:
  0.0 35.9 %sweep.1 = bf16[24,128,128]{2,1,0:T(8,128)(2,1)S(1)} custom-call(s32[8]{0:T(128)} %delays_hbm.1, s32[24]{0:T(128)} %ridge_hbm.1, bf16[768,2048]{1,0:T(8,128)(2,1)} %hidden_ref.1, bf16[768,128]{1,0:T(8,128)(2,1)} %bold_ref.1, bf16[4,4096]{1,0:T(4,128)(2,1)} %bitcast.3, s32[1,3072]{1,0:T(1,128)} %bitcast.4, f32[1,128]{1,0:T(1,128)} %bitcast.5), custom_call_target="tpu_custom_call" | custom-call | tf_op jit(solution)/shard_map/sweep/pallas_call | solution.py:273
  35.9 0.9 %copy.9 = bf16[24,128,128]{2,1,0:T(8,128)(2,1)} copy(bf16[24,128,128]{2,1,0:T(8,128)(2,1)S(1)} %sweep.1) | data formatting | bytes 1572864

commit v4 on v3

--- a/solution.py
+++ b/solution.py
@@ -33,7 +33,7 @@
     out_ref,
     delays_ref, ridge_ref, panel_ref, runs_ref, eig_ref, scale,
     hid, bext, wbuf, abuf, xbuf, sbuf, rbuf, masks,
-    in_sem, hid_sem, bold_sem, halo_sem, w_sem, a_sem, x_sem, r_sem, near_sem, far_sem,
+    in_sem, hid_sem, bold_sem, halo_sem, w_sem, a_sem, x_sem, r_sem, near_sem, chain_sem,
 ):
     n_v, n_f, n_t, t_rows, d_local, p_local = sizes
     d_chunk = d_local // n_t
@@ -62,10 +62,12 @@
         pl.semaphore_signal(sem, inc=1, device_id=where, device_id_type=MESH)
 
     barrier = pltpu.get_barrier_semaphore()
-    near = [at(dj=s, flip=w) for s in range(n_t) for w in (False, True) if s or w]
-    near += [at(dx=s) for s in range(1, n_x)]
-    along = [at(dz=s) for s in (-2, -1, 1, 2)]
-    for where in near + along:
+    sibling = at(flip=True)
+    tm_peers = {step: at(dj=step) for step in range(1, n_t)}
+    x_peers = [at(dx=step) for step in range(1, n_x)]
+    along = {step: at(dz=step) for step in (-2, -1, 1, 2)}
+    near = [*tm_peers.values(), *along.values(), *x_peers, sibling]
+    for where in near:
         signal(barrier, where)
 
     panel_copy = pltpu.make_async_copy(panel_hbm, panel_ref, in_sem.at[0])
@@ -102,7 +104,13 @@
         part = dot(tall[:, b * block:(b + 1) * block], squeeze)
         wbuf[j, :, pl.ds(b * LANES, LANES)] = part.astype(BF16)
 
-    pl.semaphore_wait(barrier, len(near) + len(along))
+    other_tm_peers = {step: at(dj=step, flip=True) for step in range(1, n_t)}
+    z_peers = {step: at(dz=N_ZLO * step) for step in range(1, n_f)}
+    window = [
+        at(dx=dx, dz=dz) for dx in (2, 1, 3, 0) for dz in (-2, -1, 1, 0) if dx or dz
+    ]
+
+    pl.semaphore_wait(barrier, len(near))
 
     def remote(src, dst, sems, slot, where):
         return pltpu.make_async_remote_copy(
@@ -110,10 +118,11 @@
             device_id=where, device_id_type=MESH,
         )
 
-    w_sends = [remote(wbuf.at[j], wbuf.at[j], w_sem, s - 1, at(dj=s)) for s in range(1, n_t)]
-    for copy in w_sends:
+    w_sends = {s: remote(wbuf.at[j], wbuf.at[j], w_sem, s - 1, tm_peers[s]) for s in (2, 1, 3)}
+    for copy in w_sends.values():
         copy.start()
-    for where in along:
+    signal(chain_sem.at[0], along[2])
+    for where in (*along.values(), sibling):
         signal(near_sem, where)
     tail = HALF * 2 - t_rows - 16
     for c in range(2):
@@ -121,17 +130,17 @@
     halos = [
         remote(
             bold_ref.at[pl.ds(0, 16)], bext.at[core, pl.ds(t_rows, 16)],
-            halo_sem, s, at(dj=n_t - 1, flip=s == 1),
+            halo_sem, s, (other_tm_peers if s else tm_peers)[n_t - 1],
         )
         for s in range(2)
     ]
     share = pltpu.make_async_remote_copy(
         src_ref=bold_ref, dst_ref=bext.at[core, pl.ds(0, t_rows)],
         send_sem=bold_sem.at[1], recv_sem=bold_sem.at[2],
-        device_id=at(flip=True), device_id_type=MESH,
+        device_id=sibling, device_id_type=MESH,
     )
-    for copy in halos + [share]:
-        copy.start()
+    halos[0].start()
+    share.start()
 
     runs_copy.wait()
     own_runs = runs_ref[:, pl.ds(pl.multiple_of(j * t_rows, LANES), t_rows)]
@@ -143,9 +152,8 @@
         same = (pltpu.roll(runs, m, 1) == runs) & inside
         masks[m - 1] = jnp.where(same, 1.0, 0.0)
 
-    pl.semaphore_wait(near_sem, len(along))
-    for where in (at(dz=-4), at(dz=4)):
-        signal(far_sem, where)
+    pl.semaphore_wait(chain_sem.at[0], 1)
+    signal(chain_sem.at[1], along[2])
 
     delays_copy.wait()
     shape = (8 * MAXD, n_rows)
@@ -163,7 +171,10 @@
     nt = ((1,), (1,))
     g = dot(wbuf[j], hid[j], nt)
     for s in (1, 3, 2):
-        w_sends[s - 1].wait_recv()
+        if s == 2:
+            pl.semaphore_wait(chain_sem.at[1], 1)
+            signal(chain_sem.at[2], along[2])
+        w_sends[s].wait_recv()
         source = lax.rem(j + n_t - s, n_t)
         g = g + dot(wbuf[source], hid[source], nt)
 
@@ -178,10 +189,13 @@
     second = jnp.concatenate([gs[:, HALF:], jnp.zeros((8, 2 * HALF - ext), F32)], 1)
     low_rows = iota((8, HALF), 0) < p_local
     abuf[f] = jnp.where(low_rows, gs[:, :HALF], second).astype(BF16)
-    pl.semaphore_wait(far_sem, 2)
-    a_sends = [remote(abuf.at[f], abuf.at[f], a_sem, s - 1, at(dz=N_ZLO * s)) for s in (2, 1, 3)]
-    for copy in a_sends:
-        copy.start()
+    a_sends = {s: remote(abuf.at[f], abuf.at[f], a_sem, s - 1, z_peers[s]) for s in (1, 3, 2)}
+    pl.semaphore_wait(near_sem, len(along) + 1)
+    a_sends[1].start()
+    a_sends[3].start()
+    pl.semaphore_wait(chain_sem.at[2], 1)
+    a_sends[2].start()
+    halos[1].start()
 
     ridge_copy.wait()
     eig_copy.wait()
@@ -196,19 +210,18 @@
         return carry
 
     lax.fori_loop(0, RIDGES, factor, 0)
-    for copy in a_sends:
+    for copy in a_sends.values():
         copy.wait_recv()
     total = abuf[0].astype(F32)
     for s in range(1, n_f):
         total = total + abuf[s].astype(F32)
     xbuf[chip] = total.astype(BF16)
 
-    steps = [(dx, dz) for dx in (2, 1, 3, 0) for dz in (-2, -1, 1, 0) if dx or dz]
-    for dx, dz in steps:
+    for where in window:
         pltpu.make_async_remote_copy(
             src_ref=xbuf.at[chip], dst_ref=xbuf.at[chip],
             send_sem=x_sem.at[0], recv_sem=x_sem.at[1],
-            device_id=at(dx=dx, dz=dz), device_id_type=MESH,
+            device_id=where, device_id_type=MESH,
         ).start()
     for copy in halos + [share]:
         copy.wait_recv()
@@ -230,11 +243,11 @@
         for c in range(2):
             sbuf[c, pl.ds(8 * g2, 8), :] = r[:, c * LANES:(c + 1) * LANES]
     rbuf[j, core] = sbuf[core]
+    order = [(2, 1), (2, 0), (1, 1), (3, 1), (1, 0), (3, 0), (0, 1)]
     r_sends = []
-    for n, (s, w) in enumerate(((2, True), (2, False), (1, True), (3, True), (1, False), (3, False), (0, True))):
-        r_sends.append(
-            remote(sbuf.at[1 - core if w else core], rbuf.at[j, core], r_sem, n, at(dj=s, flip=w))
-        )
+    for n, (s, w) in enumerate(order):
+        where = sibling if s == 0 else (other_tm_peers if w else tm_peers)[s]
+        r_sends.append(remote(sbuf.at[1 - core if w else core], rbuf.at[j, core], r_sem, n, where))
     for copy in r_sends:
         copy.start()
     for copy in r_sends:
@@ -255,7 +268,7 @@
     for n in range(RIDGES):
         out_ref[n] = (rotated * scale[n]).astype(BF16)
 
-    for copy in w_sends + a_sends + r_sends + halos + [share]:
+    for copy in [*w_sends.values(), *a_sends.values(), *r_sends, *halos, share]:
         copy.wait_send()
     pltpu.make_async_copy(arrived, arrived, x_sem.at[0]).wait()
 
@@ -299,7 +312,7 @@
             dma((2,)),
             dma((2, 2 * n_t - 1)),
             pltpu.SemaphoreType.REGULAR,
-            pltpu.SemaphoreType.REGULAR,
+            pltpu.SemaphoreType.REGULAR((3,)),
         ],
         compiler_params=pltpu.CompilerParams(collective_id=0, has_side_effects=True),
         name="sweep",

time: 36.9 us -> 37.4 us (1.014)
  Pallas kernels: 35.9 us -> 36.4 us
    pallas_call x1, Pallas kernels: 35.9 us -> 36.4 us  [shards(): pl.pallas_call(functools.partial(kernel, (n_v, n_f, n_t, t_rows, d_local,...]
where the time goes in v4:
time: 37.4 us; the launch traced here: 37.3 us
  Pallas kernels  36.4 us (97%)
  local copies, waits for them, and re-layouts  0.88 us (2%)
    pallas_call x1, Pallas kernels, shards(): pl.pallas_call(functools.partial(kernel, (n_v, n_f, n_t, t_rows, d_local,...  36.4 us
    unnamed x1, local copies, waits for them, and re-layouts  0.88 us

profile of v4, /device:TPU:1, one launch (start us, length us, event | category | flops | bytes accessed | tf_op | source)
XLA Modules:
  0.0 37.3 jit_solution(3510422126408242567)
XLA Ops:
  0.0 36.4 %sweep.1 = bf16[24,128,128]{2,1,0:T(8,128)(2,1)S(1)} custom-call(s32[8]{0:T(128)} %delays_hbm.1, s32[24]{0:T(128)} %ridge_hbm.1, bf16[768,2048]{1,0:T(8,128)(2,1)} %hidden_ref.1, bf16[768,128]{1,0:T(8,128)(2,1)} %bold_ref.1, bf16[4,4096]{1,0:T(4,128)(2,1)} %bitcast.3, s32[1,3072]{1,0:T(1,128)} %bitcast.4, f32[1,128]{1,0:T(1,128)} %bitcast.5), custom_call_target="tpu_custom_call" | custom-call | tf_op jit(solution)/shard_map/sweep/pallas_call | solution.py:286
  36.4 0.9 %copy.9 = bf16[24,128,128]{2,1,0:T(8,128)(2,1)} copy(bf16[24,128,128]{2,1,0:T(8,128)(2,1)S(1)} %sweep.1) | data formatting | bytes 1572864

commit v5 on v4

--- a/solution.py
+++ b/solution.py
@@ -32,8 +32,8 @@
     delays_hbm, ridge_hbm, hidden_ref, bold_ref, panel_hbm, runs_hbm, eig_hbm,
     out_ref,
     delays_ref, ridge_ref, panel_ref, runs_ref, eig_ref, scale,
-    hid, bext, wbuf, abuf, xbuf, sbuf, rbuf, masks,
-    in_sem, hid_sem, bold_sem, halo_sem, w_sem, a_sem, x_sem, r_sem, near_sem, chain_sem,
+    hid, bext, wbuf, gbuf, abuf, xbuf, sbuf, rbuf, masks,
+    in_sem, hid_sem, bold_sem, halo_sem, w_sem, a_sem, x_sem, r_sem, near_sem, far_sem,
 ):
     n_v, n_f, n_t, t_rows, d_local, p_local = sizes
     d_chunk = d_local // n_t
@@ -46,7 +46,7 @@
     core = lax.rem(i, 2)
     x = i // (2 * N_ZLO)
     z = f * N_ZLO + lax.rem(i // 2, N_ZLO)
-    chip = i // 2
+    chip = x * N_ZLO + lax.rem(z + 2, N_ZLO)
 
     def at(dx=0, dz=0, dj=0, flip=False):
         xx = lax.rem(x + dx, n_x)
@@ -62,13 +62,17 @@
         pl.semaphore_signal(sem, inc=1, device_id=where, device_id_type=MESH)
 
     barrier = pltpu.get_barrier_semaphore()
+    tm_peers, along = {}, {}
+    for step in (2, 1, 3):
+        tm_peers[step] = at(dj=step)
+        signal(barrier, tm_peers[step])
+    for step in (2, -2, 1, -1):
+        along[step] = at(dz=step)
+        signal(barrier, along[step])
     sibling = at(flip=True)
-    tm_peers = {step: at(dj=step) for step in range(1, n_t)}
-    x_peers = [at(dx=step) for step in range(1, n_x)]
-    along = {step: at(dz=step) for step in (-2, -1, 1, 2)}
-    near = [*tm_peers.values(), *along.values(), *x_peers, sibling]
-    for where in near:
-        signal(barrier, where)
+    signal(barrier, sibling)
+    for step in range(1, n_x):
+        signal(barrier, at(dx=step))
 
     panel_copy = pltpu.make_async_copy(panel_hbm, panel_ref, in_sem.at[0])
     runs_copy = pltpu.make_async_copy(runs_hbm, runs_ref, in_sem.at[1])
@@ -105,12 +109,12 @@
         wbuf[j, :, pl.ds(b * LANES, LANES)] = part.astype(BF16)
 
     other_tm_peers = {step: at(dj=step, flip=True) for step in range(1, n_t)}
-    z_peers = {step: at(dz=N_ZLO * step) for step in range(1, n_f)}
+    z_peers = {step: along[step] if step in along else at(dz=step) for step in (6, -6, 2, -2)}
     window = [
         at(dx=dx, dz=dz) for dx in (2, 1, 3, 0) for dz in (-2, -1, 1, 0) if dx or dz
     ]
 
-    pl.semaphore_wait(barrier, len(near))
+    pl.semaphore_wait(barrier, len(tm_peers) + len(along) + n_x)
 
     def remote(src, dst, sems, slot, where):
         return pltpu.make_async_remote_copy(
@@ -121,7 +125,6 @@
     w_sends = {s: remote(wbuf.at[j], wbuf.at[j], w_sem, s - 1, tm_peers[s]) for s in (2, 1, 3)}
     for copy in w_sends.values():
         copy.start()
-    signal(chain_sem.at[0], along[2])
     for where in (*along.values(), sibling):
         signal(near_sem, where)
     tail = HALF * 2 - t_rows - 16
@@ -152,8 +155,9 @@
         same = (pltpu.roll(runs, m, 1) == runs) & inside
         masks[m - 1] = jnp.where(same, 1.0, 0.0)
 
-    pl.semaphore_wait(chain_sem.at[0], 1)
-    signal(chain_sem.at[1], along[2])
+    pl.semaphore_wait(near_sem, len(along) + 1)
+    signal(far_sem, along[2])
+    signal(far_sem, along[-2])
 
     delays_copy.wait()
     shape = (8 * MAXD, n_rows)
@@ -171,9 +175,6 @@
     nt = ((1,), (1,))
     g = dot(wbuf[j], hid[j], nt)
     for s in (1, 3, 2):
-        if s == 2:
-            pl.semaphore_wait(chain_sem.at[1], 1)
-            signal(chain_sem.at[2], along[2])
         w_sends[s].wait_recv()
         source = lax.rem(j + n_t - s, n_t)
         g = g + dot(wbuf[source], hid[source], nt)
@@ -188,13 +189,13 @@
 
     second = jnp.concatenate([gs[:, HALF:], jnp.zeros((8, 2 * HALF - ext), F32)], 1)
     low_rows = iota((8, HALF), 0) < p_local
-    abuf[f] = jnp.where(low_rows, gs[:, :HALF], second).astype(BF16)
-    a_sends = {s: remote(abuf.at[f], abuf.at[f], a_sem, s - 1, z_peers[s]) for s in (1, 3, 2)}
-    pl.semaphore_wait(near_sem, len(along) + 1)
-    a_sends[1].start()
-    a_sends[3].start()
-    pl.semaphore_wait(chain_sem.at[2], 1)
-    a_sends[2].start()
+    gbuf[...] = jnp.where(low_rows, gs[:, :HALF], second).astype(BF16)
+    a_sends = [
+        remote(gbuf, abuf.at[f], a_sem, n, where) for n, where in enumerate(z_peers.values())
+    ]
+    pl.semaphore_wait(far_sem, 2)
+    for copy in a_sends:
+        copy.start()
     halos[1].start()
 
     ridge_copy.wait()
@@ -210,7 +211,7 @@
         return carry
 
     lax.fori_loop(0, RIDGES, factor, 0)
-    for copy in a_sends.values():
+    for copy in a_sends:
         copy.wait_recv()
     total = abuf[0].astype(F32)
     for s in range(1, n_f):
@@ -268,7 +269,7 @@
     for n in range(RIDGES):
         out_ref[n] = (rotated * scale[n]).astype(BF16)
 
-    for copy in [*w_sends.values(), *a_sends.values(), *r_sends, *halos, share]:
+    for copy in [*w_sends.values(), *a_sends, *r_sends, *halos, share]:
         copy.wait_send()
     pltpu.make_async_copy(arrived, arrived, x_sem.at[0]).wait()
 
@@ -298,6 +299,7 @@
             pltpu.VMEM((n_t, t_rows, d_chunk), BF16),
             pltpu.VMEM((2, 2 * HALF, v_cols), BF16),
             pltpu.VMEM((n_t, DELAYS * p_local, d_chunk), BF16),
+            pltpu.VMEM((8, HALF), BF16),
             pltpu.VMEM((n_f, 8, HALF), BF16),
             pltpu.VMEM((n_v // 2, 8, HALF), BF16),
             pltpu.VMEM((2, n_v * 2, v_cols), BF16),
@@ -308,11 +310,11 @@
             dma((3,)),
             dma((2, 2)),
             dma((2, n_t - 1)),
-            dma((2, n_f - 1)),
+            dma((2, n_f)),
             dma((2,)),
             dma((2, 2 * n_t - 1)),
             pltpu.SemaphoreType.REGULAR,
-            pltpu.SemaphoreType.REGULAR((3,)),
+            pltpu.SemaphoreType.REGULAR,
         ],
         compiler_params=pltpu.CompilerParams(collective_id=0, has_side_effects=True),
         name="sweep",

time: 37.4 us -> 35 us (0.936)
  Pallas kernels: 36.4 us -> 34 us
    pallas_call x1, Pallas kernels: 36.4 us -> 34 us  [shards(): pl.pallas_call(functools.partial(kernel, (n_v, n_f, n_t, t_rows, d_local,...]
where the time goes in v5:
time: 35 us; the launch traced here: 34.9 us
  Pallas kernels  34 us (97%)
  local copies, waits for them, and re-layouts  0.88 us (3%)
    pallas_call x1, Pallas kernels, shards(): pl.pallas_call(functools.partial(kernel, (n_v, n_f, n_t, t_rows, d_local,...  34 us
    unnamed x1, local copies, waits for them, and re-layouts  0.88 us

profile of v5, /device:TPU:1, one launch (start us, length us, event | category | flops | bytes accessed | tf_op | source)
XLA Modules:
  0.0 34.9 jit_solution(14949383134871473072)
XLA Ops:
  0.0 34.0 %sweep.1 = bf16[24,128,128]{2,1,0:T(8,128)(2,1)S(1)} custom-call(s32[8]{0:T(128)} %delays_hbm.1, s32[24]{0:T(128)} %ridge_hbm.1, bf16[768,2048]{1,0:T(8,128)(2,1)} %hidden_ref.1, bf16[768,128]{1,0:T(8,128)(2,1)} %bold_ref.1, bf16[4,4096]{1,0:T(4,128)(2,1)} %bitcast.3, s32[1,3072]{1,0:T(1,128)} %bitcast.4, f32[1,128]{1,0:T(1,128)} %bitcast.5), custom_call_target="tpu_custom_call" | custom-call | tf_op jit(solution)/shard_map/sweep/pallas_call | solution.py:287
  34.1 0.9 %copy.9 = bf16[24,128,128]{2,1,0:T(8,128)(2,1)} copy(bf16[24,128,128]{2,1,0:T(8,128)(2,1)S(1)} %sweep.1) | data formatting | bytes 1572864

commit v6 on v5

--- a/solution.py
+++ b/solution.py
@@ -14,6 +14,7 @@
 LANES = 128
 HALF = 512
 N_ZLO = 4
+COLUMNS = (0, 1, 3, 2)
 BF16 = jnp.bfloat16
 F32 = jnp.float32
 MESH = pl.DeviceIdType.MESH
@@ -46,7 +47,7 @@
     core = lax.rem(i, 2)
     x = i // (2 * N_ZLO)
     z = f * N_ZLO + lax.rem(i // 2, N_ZLO)
-    chip = x * N_ZLO + lax.rem(z + 2, N_ZLO)
+    z_sum = lax.rem(z + 2, N_ZLO)
 
     def at(dx=0, dz=0, dj=0, flip=False):
         xx = lax.rem(x + dx, n_x)
@@ -111,7 +112,8 @@
     other_tm_peers = {step: at(dj=step, flip=True) for step in range(1, n_t)}
     z_peers = {step: along[step] if step in along else at(dz=step) for step in (6, -6, 2, -2)}
     window = [
-        at(dx=dx, dz=dz) for dx in (2, 1, 3, 0) for dz in (-2, -1, 1, 0) if dx or dz
+        (COLUMNS.index((n_x - dx) % n_x), at(dx=dx, dz=dz))
+        for dx in (2, 1, 3, 0) for dz in (-2, -1, 1, 0) if dx or dz
     ]
 
     pl.semaphore_wait(barrier, len(tm_peers) + len(along) + n_x)
@@ -216,62 +218,86 @@
     total = abuf[0].astype(F32)
     for s in range(1, n_f):
         total = total + abuf[s].astype(F32)
-    xbuf[chip] = total.astype(BF16)
-
-    for where in window:
+    xbuf[z_sum] = total.astype(BF16)
+
+    early = N_ZLO * (n_x - 1)
+    for column, where in window:
         pltpu.make_async_remote_copy(
-            src_ref=xbuf.at[chip], dst_ref=xbuf.at[chip],
-            send_sem=x_sem.at[0], recv_sem=x_sem.at[1],
+            src_ref=xbuf.at[z_sum], dst_ref=xbuf.at[column * N_ZLO + z_sum],
+            send_sem=x_sem.at[0], recv_sem=x_sem.at[1 if column < n_x - 1 else 2],
             device_id=where, device_id_type=MESH,
         ).start()
     for copy in halos + [share]:
         copy.wait_recv()
     bold_copy.wait()
-    arrived = xbuf.at[pl.ds(0, n_v // 2 - 1)]
+
+    halves = [
+        jnp.concatenate([bext[c, pl.ds(h * HALF, HALF), :] for c in range(2)], 1) for h in range(2)
+    ]
+    order = [(2, 1), (2, 0), (1, 1), (3, 1), (1, 0), (3, 0), (0, 1)]
+
+    def multiply_and_send(first, count, slot):
+        sums = xbuf[first:first + count].reshape(count * 8, HALF)
+        both = [dot(sums, half) for half in halves]
+        upper = iota((8, 2 * LANES), 0) < p_local
+        for g2 in range(count // 2):
+            a, b = slice(16 * g2, 16 * g2 + 8), slice(16 * g2 + 8, 16 * g2 + 16)
+            u = jnp.where(upper, both[0][a], both[1][b])
+            w = jnp.where(upper, both[0][b], both[1][a])
+            r = (u + pltpu.roll(w, 4, 0)).astype(BF16)
+            for c in range(2):
+                sbuf[c, pl.ds(4 * first + 8 * g2, 8), :] = r[:, c * LANES:(c + 1) * LANES]
+        rows = pl.ds(4 * first, 4 * count)
+        copies = []
+        for n, (s, w) in enumerate(order):
+            where = sibling if s == 0 else (other_tm_peers if w else tm_peers)[s]
+            copies.append(
+                remote(
+                    sbuf.at[1 - core if w else core, rows], rbuf.at[j, core, rows],
+                    r_sem, slot + n, where,
+                )
+            )
+        for copy in copies:
+            copy.start()
+        rbuf[j, core, rows] = sbuf[core, rows]
+        return copies
+
+    arrived = xbuf.at[pl.ds(0, early - 1)]
     pltpu.make_async_copy(arrived, arrived, x_sem.at[1]).wait()
-
-    sums = xbuf[...].reshape(n_v // 2 * 8, HALF)
-    halves = []
-    for h in range(2):
-        both = jnp.concatenate([bext[c, pl.ds(h * HALF, HALF), :] for c in range(2)], 1)
-        halves.append(dot(sums, both))
-    upper = iota((8, 2 * LANES), 0) < p_local
-    for g2 in range(n_v // 4):
-        a, b = slice(16 * g2, 16 * g2 + 8), slice(16 * g2 + 8, 16 * g2 + 16)
-        u = jnp.where(upper, halves[0][a], halves[1][b])
-        w = jnp.where(upper, halves[0][b], halves[1][a])
-        r = (u + pltpu.roll(w, 4, 0)).astype(BF16)
-        for c in range(2):
-            sbuf[c, pl.ds(8 * g2, 8), :] = r[:, c * LANES:(c + 1) * LANES]
-    rbuf[j, core] = sbuf[core]
-    order = [(2, 1), (2, 0), (1, 1), (3, 1), (1, 0), (3, 0), (0, 1)]
-    r_sends = []
-    for n, (s, w) in enumerate(order):
-        where = sibling if s == 0 else (other_tm_peers if w else tm_peers)[s]
-        r_sends.append(remote(sbuf.at[1 - core if w else core], rbuf.at[j, core], r_sem, n, where))
-    for copy in r_sends:
-        copy.start()
-    for copy in r_sends:
-        copy.wait_recv()
-    upper = iota((8, LANES), 0) < p_local
-    parts = []
-    for c in range(2):
-        r = rbuf[0, c].astype(F32)
-        for s in range(1, n_t):
-            r = r + rbuf[s, c].astype(F32)
-        parts.append(r)
-    tiles = []
-    for g2 in range(n_v // 4):
-        v0, v1 = parts[0][8 * g2:8 * g2 + 8], parts[1][8 * g2:8 * g2 + 8]
-        tiles.append(jnp.where(upper, v0, pltpu.roll(v1, 4, 0)))
-        tiles.append(jnp.where(upper, pltpu.roll(v0, 4, 0), v1))
-    rotated = jnp.concatenate(tiles, 0)
-    for n in range(RIDGES):
-        out_ref[n] = (rotated * scale[n]).astype(BF16)
-
-    for copy in [*w_sends.values(), *a_sends, *r_sends, *halos, share]:
+    r_sends = multiply_and_send(0, early, 0)
+    arrived = xbuf.at[pl.ds(0, N_ZLO)]
+    pltpu.make_async_copy(arrived, arrived, x_sem.at[2]).wait()
+    last_sends = multiply_and_send(early, N_ZLO, len(order))
+
+    def finish(copies, first, columns):
+        for copy in copies:
+            copy.wait_recv()
+        upper = iota((8, LANES), 0) < p_local
+        for q in range(first, first + columns):
+            parts = []
+            for c in range(2):
+                rows = pl.ds(16 * q, 16)
+                r = rbuf[0, c, rows].astype(F32)
+                for s in range(1, n_t):
+                    r = r + rbuf[s, c, rows].astype(F32)
+                parts.append(r)
+            tiles = []
+            for g2 in range(2):
+                v0, v1 = parts[0][8 * g2:8 * g2 + 8], parts[1][8 * g2:8 * g2 + 8]
+                tiles.append(jnp.where(upper, v0, pltpu.roll(v1, 4, 0)))
+                tiles.append(jnp.where(upper, pltpu.roll(v0, 4, 0), v1))
+            rotated = jnp.concatenate(tiles, 0)
+            span = pl.ds(pl.multiple_of(lax.rem(x + COLUMNS[q], n_x) * 32, 32), 32)
+            for n in range(RIDGES):
+                out_ref[n, span, :] = (rotated * scale[n, span, :]).astype(BF16)
+
+    finish(r_sends, 0, n_x - 1)
+    finish(last_sends, n_x - 1, 1)
+
+    for copy in [*w_sends.values(), *a_sends, *r_sends, *last_sends, *halos, share]:
         copy.wait_send()
-    pltpu.make_async_copy(arrived, arrived, x_sem.at[0]).wait()
+    sent = xbuf.at[pl.ds(0, n_v // 2 - 1)]
+    pltpu.make_async_copy(sent, sent, x_sem.at[0]).wait()
 
 
 def shards(hidden, bold, panel, eigvals, ridge_grid, delays, runs):
@@ -311,8 +337,8 @@
             dma((2, 2)),
             dma((2, n_t - 1)),
             dma((2, n_f)),
-            dma((2,)),
-            dma((2, 2 * n_t - 1)),
+            dma((3,)),
+            dma((2, 4 * n_t - 2)),
             pltpu.SemaphoreType.REGULAR,
             pltpu.SemaphoreType.REGULAR,
         ],

time: 35 us -> 35.4 us (1.011)
  Pallas kernels: 34 us -> 34.4 us
where the time goes in v6:
time: 35.4 us; the launch traced here: 35.3 us
  Pallas kernels  34.4 us (97%)
  local copies, waits for them, and re-layouts  0.88 us (2%)
    pallas_call x1, Pallas kernels, shards(): pl.pallas_call(functools.partial(kernel, (n_v, n_f, n_t, t_rows, d_local,...  34.4 us
    unnamed x1, local copies, waits for them, and re-layouts  0.88 us

profile of v6, /device:TPU:1, one launch (start us, length us, event | category | flops | bytes accessed | tf_op | source)
XLA Modules:
  0.0 35.3 jit_solution(12498438219034404139)
XLA Ops:
  0.0 34.4 %sweep.1 = bf16[24,128,128]{2,1,0:T(8,128)(2,1)S(1)} custom-call(s32[8]{0:T(128)} %delays_hbm.1, s32[24]{0:T(128)} %ridge_hbm.1, bf16[768,2048]{1,0:T(8,128)(2,1)} %hidden_ref.1, bf16[768,128]{1,0:T(8,128)(2,1)} %bold_ref.1, bf16[4,4096]{1,0:T(4,128)(2,1)} %bitcast.3, s32[1,3072]{1,0:T(1,128)} %bitcast.4, f32[1,128]{1,0:T(1,128)} %bitcast.5), custom_call_target="tpu_custom_call" | custom-call | tf_op jit(solution)/shard_map/sweep/pallas_call | solution.py:313
  34.4 0.9 %copy.9 = bf16[24,128,128]{2,1,0:T(8,128)(2,1)} copy(bf16[24,128,128]{2,1,0:T(8,128)(2,1)S(1)} %sweep.1) | data formatting | bytes 1572864

commit v7 on v5

--- a/solution.py
+++ b/solution.py
@@ -32,7 +32,7 @@
     delays_hbm, ridge_hbm, hidden_ref, bold_ref, panel_hbm, runs_hbm, eig_hbm,
     out_ref,
     delays_ref, ridge_ref, panel_ref, runs_ref, eig_ref, scale,
-    hid, bext, wbuf, gbuf, abuf, xbuf, sbuf, rbuf, masks,
+    hid, bext, wbuf, gbuf, abuf, xbuf, rbuf, masks,
     in_sem, hid_sem, bold_sem, halo_sem, w_sem, a_sem, x_sem, r_sem, near_sem, far_sem,
 ):
     n_v, n_f, n_t, t_rows, d_local, p_local = sizes
@@ -46,7 +46,7 @@
     core = lax.rem(i, 2)
     x = i // (2 * N_ZLO)
     z = f * N_ZLO + lax.rem(i // 2, N_ZLO)
-    chip = x * N_ZLO + lax.rem(z + 2, N_ZLO)
+    group = (x * N_ZLO + lax.rem(z + 2, N_ZLO)) * 2 + core
 
     def at(dx=0, dz=0, dj=0, flip=False):
         xx = lax.rem(x + dx, n_x)
@@ -92,7 +92,7 @@
     ]
     for copy in hid_copies:
         copy.start()
-    bold_copy = pltpu.make_async_copy(bold_ref, bext.at[core, pl.ds(0, t_rows)], bold_sem.at[0])
+    bold_copy = pltpu.make_async_copy(bold_ref, bext.at[pl.ds(0, t_rows)], bold_sem)
     bold_copy.start()
 
     rows_local = panel_ref.shape[1]
@@ -108,10 +108,11 @@
         part = dot(tall[:, b * block:(b + 1) * block], squeeze)
         wbuf[j, :, pl.ds(b * LANES, LANES)] = part.astype(BF16)
 
-    other_tm_peers = {step: at(dj=step, flip=True) for step in range(1, n_t)}
     z_peers = {step: along[step] if step in along else at(dz=step) for step in (6, -6, 2, -2)}
+    reach = [(dx, dz) for dx in range(n_x) for dz in (-2, -1, 0, 1)]
+    reach.sort(key=lambda step: -min(step[0], n_x - step[0]) - abs(step[1]))
     window = [
-        at(dx=dx, dz=dz) for dx in (2, 1, 3, 0) for dz in (-2, -1, 1, 0) if dx or dz
+        at(dx=dx, dz=dz, flip=flip) for dx, dz in reach for flip in (True, False) if dx or dz or flip
     ]
 
     pl.semaphore_wait(barrier, len(tm_peers) + len(along) + n_x)
@@ -128,22 +129,11 @@
     for where in (*along.values(), sibling):
         signal(near_sem, where)
     tail = HALF * 2 - t_rows - 16
-    for c in range(2):
-        bext[c, pl.ds(t_rows + 16, tail), :] = jnp.zeros((tail, LANES), BF16)
-    halos = [
-        remote(
-            bold_ref.at[pl.ds(0, 16)], bext.at[core, pl.ds(t_rows, 16)],
-            halo_sem, s, (other_tm_peers if s else tm_peers)[n_t - 1],
-        )
-        for s in range(2)
-    ]
-    share = pltpu.make_async_remote_copy(
-        src_ref=bold_ref, dst_ref=bext.at[core, pl.ds(0, t_rows)],
-        send_sem=bold_sem.at[1], recv_sem=bold_sem.at[2],
-        device_id=sibling, device_id_type=MESH,
+    bext[pl.ds(t_rows + 16, tail), :] = jnp.zeros((tail, LANES), BF16)
+    halo = remote(
+        bold_ref.at[pl.ds(0, 16)], bext.at[pl.ds(t_rows, 16)], halo_sem, 0, tm_peers[n_t - 1]
     )
-    halos[0].start()
-    share.start()
+    halo.start()
 
     runs_copy.wait()
     own_runs = runs_ref[:, pl.ds(pl.multiple_of(j * t_rows, LANES), t_rows)]
@@ -158,6 +148,7 @@
     pl.semaphore_wait(near_sem, len(along) + 1)
     signal(far_sem, along[2])
     signal(far_sem, along[-2])
+    signal(far_sem, sibling)
 
     delays_copy.wait()
     shape = (8 * MAXD, n_rows)
@@ -193,10 +184,9 @@
     a_sends = [
         remote(gbuf, abuf.at[f], a_sem, n, where) for n, where in enumerate(z_peers.values())
     ]
-    pl.semaphore_wait(far_sem, 2)
+    pl.semaphore_wait(far_sem, 3)
     for copy in a_sends:
         copy.start()
-    halos[1].start()
 
     ridge_copy.wait()
     eig_copy.wait()
@@ -216,60 +206,39 @@
     total = abuf[0].astype(F32)
     for s in range(1, n_f):
         total = total + abuf[s].astype(F32)
-    xbuf[chip] = total.astype(BF16)
+    xbuf[group] = total.astype(BF16)
 
     for where in window:
         pltpu.make_async_remote_copy(
-            src_ref=xbuf.at[chip], dst_ref=xbuf.at[chip],
+            src_ref=xbuf.at[group], dst_ref=xbuf.at[group],
             send_sem=x_sem.at[0], recv_sem=x_sem.at[1],
             device_id=where, device_id_type=MESH,
         ).start()
-    for copy in halos + [share]:
-        copy.wait_recv()
+    halo.wait_recv()
     bold_copy.wait()
-    arrived = xbuf.at[pl.ds(0, n_v // 2 - 1)]
+    arrived = xbuf.at[pl.ds(0, n_v - 1)]
     pltpu.make_async_copy(arrived, arrived, x_sem.at[1]).wait()
 
-    sums = xbuf[...].reshape(n_v // 2 * 8, HALF)
-    halves = []
-    for h in range(2):
-        both = jnp.concatenate([bext[c, pl.ds(h * HALF, HALF), :] for c in range(2)], 1)
-        halves.append(dot(sums, both))
-    upper = iota((8, 2 * LANES), 0) < p_local
-    for g2 in range(n_v // 4):
+    sums = xbuf[...].reshape(n_v * 8, HALF)
+    halves = [dot(sums, bext[pl.ds(h * HALF, HALF), :]) for h in range(2)]
+    upper = iota((8, LANES), 0) < p_local
+    for g2 in range(n_v // 2):
         a, b = slice(16 * g2, 16 * g2 + 8), slice(16 * g2 + 8, 16 * g2 + 16)
         u = jnp.where(upper, halves[0][a], halves[1][b])
         w = jnp.where(upper, halves[0][b], halves[1][a])
-        r = (u + pltpu.roll(w, 4, 0)).astype(BF16)
-        for c in range(2):
-            sbuf[c, pl.ds(8 * g2, 8), :] = r[:, c * LANES:(c + 1) * LANES]
-    rbuf[j, core] = sbuf[core]
-    order = [(2, 1), (2, 0), (1, 1), (3, 1), (1, 0), (3, 0), (0, 1)]
-    r_sends = []
-    for n, (s, w) in enumerate(order):
-        where = sibling if s == 0 else (other_tm_peers if w else tm_peers)[s]
-        r_sends.append(remote(sbuf.at[1 - core if w else core], rbuf.at[j, core], r_sem, n, where))
+        rbuf[j, pl.ds(8 * g2, 8), :] = (u + pltpu.roll(w, 4, 0)).astype(BF16)
+    r_sends = [remote(rbuf.at[j], rbuf.at[j], r_sem, s - 1, tm_peers[s]) for s in (2, 1, 3)]
     for copy in r_sends:
         copy.start()
     for copy in r_sends:
         copy.wait_recv()
-    upper = iota((8, LANES), 0) < p_local
-    parts = []
-    for c in range(2):
-        r = rbuf[0, c].astype(F32)
-        for s in range(1, n_t):
-            r = r + rbuf[s, c].astype(F32)
-        parts.append(r)
-    tiles = []
-    for g2 in range(n_v // 4):
-        v0, v1 = parts[0][8 * g2:8 * g2 + 8], parts[1][8 * g2:8 * g2 + 8]
-        tiles.append(jnp.where(upper, v0, pltpu.roll(v1, 4, 0)))
-        tiles.append(jnp.where(upper, pltpu.roll(v0, 4, 0), v1))
-    rotated = jnp.concatenate(tiles, 0)
+    rotated = rbuf[0].astype(F32)
+    for s in range(1, n_t):
+        rotated = rotated + rbuf[s].astype(F32)
     for n in range(RIDGES):
         out_ref[n] = (rotated * scale[n]).astype(BF16)
 
-    for copy in [*w_sends.values(), *a_sends, *r_sends, *halos, share]:
+    for copy in [*w_sends.values(), *a_sends, *r_sends, halo]:
         copy.wait_send()
     pltpu.make_async_copy(arrived, arrived, x_sem.at[0]).wait()
 
@@ -297,22 +266,21 @@
             pltpu.VMEM((1, n_p), F32),
             pltpu.VMEM((RIDGES, n_p, v_cols), F32),
             pltpu.VMEM((n_t, t_rows, d_chunk), BF16),
-            pltpu.VMEM((2, 2 * HALF, v_cols), BF16),
+            pltpu.VMEM((2 * HALF, v_cols), BF16),
             pltpu.VMEM((n_t, DELAYS * p_local, d_chunk), BF16),
             pltpu.VMEM((8, HALF), BF16),
             pltpu.VMEM((n_f, 8, HALF), BF16),
-            pltpu.VMEM((n_v // 2, 8, HALF), BF16),
-            pltpu.VMEM((2, n_v * 2, v_cols), BF16),
-            pltpu.VMEM((n_t, 2, n_v * 2, v_cols), BF16),
+            pltpu.VMEM((n_v, 8, HALF), BF16),
+            pltpu.VMEM((n_t, n_p, v_cols), BF16),
             pltpu.VMEM((MAXD, 8, ext), F32),
             dma((5,)),
             dma((n_t,)),
-            dma((3,)),
-            dma((2, 2)),
+            dma,
+            dma((2, 1)),
             dma((2, n_t - 1)),
             dma((2, n_f)),
             dma((2,)),
-            dma((2, 2 * n_t - 1)),
+            dma((2, n_t - 1)),
             pltpu.SemaphoreType.REGULAR,
             pltpu.SemaphoreType.REGULAR,
         ],

time: 35 us -> 35 us (level)
  no operation moved by 1% of the time
where the time goes in v7:
time: 35 us; the launch traced here: 34.9 us
  Pallas kernels  34 us (97%)
  local copies, waits for them, and re-layouts  0.88 us (3%)
    pallas_call x1, Pallas kernels, shards(): pl.pallas_call(functools.partial(kernel, (n_v, n_f, n_t, t_rows, d_local,...  34 us
    unnamed x1, local copies, waits for them, and re-layouts  0.88 us

profile of v7, /device:TPU:1, one launch (start us, length us, event | category | flops | bytes accessed | tf_op | source)
XLA Modules:
  0.0 34.9 jit_solution(9859605432547161690)
XLA Ops:
  0.0 34.0 %sweep.1 = bf16[24,128,128]{2,1,0:T(8,128)(2,1)S(1)} custom-call(s32[8]{0:T(128)} %delays_hbm.1, s32[24]{0:T(128)} %ridge_hbm.1, bf16[768,2048]{1,0:T(8,128)(2,1)} %hidden_ref.1, bf16[768,128]{1,0:T(8,128)(2,1)} %bold_ref.1, bf16[4,4096]{1,0:T(4,128)(2,1)} %bitcast.3, s32[1,3072]{1,0:T(1,128)} %bitcast.4, f32[1,128]{1,0:T(1,128)} %bitcast.5), custom_call_target="tpu_custom_call" | custom-call | tf_op jit(solution)/shard_map/sweep/pallas_call | solution.py:256
  34.0 0.9 %copy.9 = bf16[24,128,128]{2,1,0:T(8,128)(2,1)} copy(bf16[24,128,128]{2,1,0:T(8,128)(2,1)S(1)} %sweep.1) | data formatting | bytes 1572864

commit v8 on v7

--- a/solution.py
+++ b/solution.py
@@ -220,7 +220,9 @@
     pltpu.make_async_copy(arrived, arrived, x_sem.at[1]).wait()
 
     sums = xbuf[...].reshape(n_v * 8, HALF)
-    halves = [dot(sums, bext[pl.ds(h * HALF, HALF), :]) for h in range(2)]
+    wide = jnp.concatenate([bext[pl.ds(h * HALF, HALF), :] for h in range(2)], 1)
+    product = dot(sums, wide)
+    halves = [product[:, h * LANES:(h + 1) * LANES] for h in range(2)]
     upper = iota((8, LANES), 0) < p_local
     for g2 in range(n_v // 2):
         a, b = slice(16 * g2, 16 * g2 + 8), slice(16 * g2 + 8, 16 * g2 + 16)

time: 35 us -> 34.8 us (level)
  no operation moved by 1% of the time
where the time goes in v8:
time: 34.8 us; the launch traced here: 34.7 us
  Pallas kernels  33.8 us (97%)
  local copies, waits for them, and re-layouts  0.88 us (3%)
    pallas_call x1, Pallas kernels, shards(): pl.pallas_call(functools.partial(kernel, (n_v, n_f, n_t, t_rows, d_local,...  33.8 us
    unnamed x1, local copies, waits for them, and re-layouts  0.88 us

profile of v8, /device:TPU:1, one launch (start us, length us, event | category | flops | bytes accessed | tf_op | source)
XLA Modules:
  0.0 34.7 jit_solution(3427573537265505052)
XLA Ops:
  0.0 33.8 %sweep.1 = bf16[24,128,128]{2,1,0:T(8,128)(2,1)S(1)} custom-call(s32[8]{0:T(128)} %delays_hbm.1, s32[24]{0:T(128)} %ridge_hbm.1, bf16[768,2048]{1,0:T(8,128)(2,1)} %hidden_ref.1, bf16[768,128]{1,0:T(8,128)(2,1)} %bold_ref.1, bf16[4,4096]{1,0:T(4,128)(2,1)} %bitcast.3, s32[1,3072]{1,0:T(1,128)} %bitcast.4, f32[1,128]{1,0:T(1,128)} %bitcast.5), custom_call_target="tpu_custom_call" | custom-call | tf_op jit(solution)/shard_map/sweep/pallas_call | solution.py:258
  33.9 0.9 %copy.9 = bf16[24,128,128]{2,1,0:T(8,128)(2,1)} copy(bf16[24,128,128]{2,1,0:T(8,128)(2,1)S(1)} %sweep.1) | data formatting | bytes 1572864
